TPU v7x, 32 devices: a whole 2x2x4 slice. The times are simulated.
32 devices in a mesh: ia: 4 (over z), ja: 4 (over y, x), ka: 2 (over core).
Axes of the slice: x: 2, y: 2, z: 4, core: 2. Of those that a mesh axis runs over, the one named last changes fastest.
Arguments:
- blocks: bfloat16 [4, 4, 4, 128, 128, 128], P('ia', 'ja', 'ka'), may hold values from -6 to 6
- coordinates: int32 [3, 4, 4, 4], P(None, 'ia', 'ja', 'ka'), may hold values from 0 to 3, as said below
- occupancy: int32 [4, 4, 4], P('ia', 'ja', 'ka'), may hold values from 0 to 1, as said below
- second_factor: bfloat16 [4, 512, 1024], P('ja', ('ia', 'ka')), may hold values from -12 to 12
- third_factor: bfloat16 [2, 512, 1024], P('ka', ('ia', 'ja')), may hold values from -0.0234375 to 0.0234375
- inverse_first: bfloat16 [1024, 1024], replicated
- inverse_second: bfloat16 [1024, 1024], replicated
Outputs:
- first_new: bfloat16 [4, 512, 1024], P('ia', ('ja', 'ka'))
- second_new: bfloat16 [4, 512, 1024], P('ja', ('ia', 'ka'))
Inputs may be any that keep to these rules, and one draw needn't show every extreme that they name: `occupancy`: each device has two slots; its second slot is occupied only where its first is. A device with two blocks is followed along ka, cyclically, by a device with none. Some device holds two blocks. coordinates[0], [1], [2] of a slot are a block row among 4, a block row among 4 and a block layer among 4 of its device's ranges; the two slots of a device name different layers.
All inputs are finite; a program needn't handle non-finite values.
Results may differ from a plain program's by a relative error of at most 0.006.
Values may be sent and summed in bfloat16 or wider, within the bound.
A program may use at most 128 MiB of HBM per device.

v0:
```python
import jax
import jax.numpy as jnp
from jax import lax
from jax.sharding import PartitionSpec as P

IB = 4
JB = 4


def passed_along(block, axis, distance):
    devices = range(lax.axis_size(axis))
    route = [((i - distance) % len(devices), i) for i in devices]
    return lax.ppermute(block, axis, route)


def block_products(tensor_block, left_rows, layer_slab, contract):
    block_edge = tensor_block.shape[0]
    step_rows = max(block_edge // 4, 1)
    summed = jnp.zeros((block_edge, left_rows.shape[1]), jnp.float32)
    for first_row in range(0, block_edge, step_rows):
        khatri = left_rows[first_row : first_row + step_rows][:, None, :] * layer_slab[None, :, :]
        if contract == 1:
            block_part = tensor_block[:, first_row : first_row + step_rows, :]
            contraction = (((1, 2), (0, 1)), ((), ()))
        else:
            block_part = tensor_block[first_row : first_row + step_rows]
            contraction = (((0, 2), (0, 1)), ((), ()))
        summed = summed + lax.dot_general(
            block_part, khatri, contraction, preferred_element_type=jnp.float32
        )
    return summed


def place_rows(partial_value, addend, block_index):
    block_edge = addend.shape[0]
    row_start = block_index * block_edge
    current = lax.dynamic_slice_in_dim(partial_value, row_start, block_edge, 0)
    return lax.dynamic_update_slice_in_dim(partial_value, addend, row_start, 0)


def pick_rows(source, block_index, block_edge):
    return lax.dynamic_slice_in_dim(source, block_index * block_edge, block_edge, 0)


def body(
    blocks, coordinates, occupancy, second_factor, third_factor, inverse_first, inverse_second
):
    block_edge = blocks.shape[-1]
    rank_width = inverse_first.shape[0]
    own_blocks = blocks.reshape(2, block_edge, block_edge, block_edge)
    places = coordinates.reshape(3, 2)
    occupied = occupancy.reshape(2)
    second_rows = lax.all_gather(second_factor, ("ia", "ka"), axis=1, tiled=True)[0]
    layer_rows = lax.all_gather(third_factor, ("ia", "ja"), axis=1, tiled=True)[0]
    slot_meta = jnp.stack([occupied[1], places[0, 1], places[1, 1]]).astype(jnp.bfloat16)
    arrived, arrived_layer, arrived_meta = passed_along(
        (own_blocks[1], pick_rows(layer_rows, places[2, 1], block_edge), slot_meta), "ka", 1
    )
    arrived_index = arrived_meta.astype(jnp.int32)
    keep_own = occupied[0] > 0
    tensor_block = jnp.where(keep_own, own_blocks[0], arrived)
    layer_slab = jnp.where(keep_own, pick_rows(layer_rows, places[2, 0], block_edge), arrived_layer)
    row_block = jnp.where(keep_own, places[0, 0], arrived_index[1])
    col_block = jnp.where(keep_own, places[1, 0], arrived_index[2])
    weight = jnp.where(keep_own, 1, arrived_index[0]).astype(jnp.float32)
    first_partial = jnp.zeros((IB * block_edge, rank_width), jnp.float32)
    contribution = block_products(
        tensor_block, pick_rows(second_rows, col_block, block_edge), layer_slab, 1
    )
    first_partial = place_rows(first_partial, contribution * weight, row_block)
    summed_rows = lax.psum(first_partial, ("ja", "ka"))
    first_rows = jnp.dot(
        summed_rows.astype(jnp.bfloat16), inverse_first, preferred_element_type=jnp.float32
    ).astype(jnp.bfloat16)
    share_rows = first_rows.shape[0] // lax.axis_size(("ja", "ka"))
    first_new = lax.dynamic_slice_in_dim(
        first_rows, lax.axis_index(("ja", "ka")) * share_rows, share_rows, 0
    )
    second_partial = jnp.zeros((JB * block_edge, rank_width), jnp.float32)
    contribution = block_products(
        tensor_block, pick_rows(first_rows, row_block, block_edge), layer_slab, 0
    )
    second_partial = place_rows(second_partial, contribution * weight, col_block)
    owned_second = lax.psum_scatter(
        second_partial[None], ("ia", "ka"), scatter_dimension=1, tiled=True
    )[0]
    second_new = jnp.dot(
        owned_second.astype(jnp.bfloat16), inverse_second, preferred_element_type=jnp.float32
    ).astype(jnp.bfloat16)
    return (first_new[None], second_new[None])


def solution(mesh):
    in_specs = (
        P("ia", "ja", "ka", None, None, None),
        P(None, "ia", "ja", "ka"),
        P("ia", "ja", "ka"),
        P("ja", ("ia", "ka"), None),
        P("ka", ("ia", "ja"), None),
        P(),
        P(),
    )
    out_specs = (P("ia", ("ja", "ka"), None), P("ja", ("ia", "ka"), None))
    return jax.shard_map(body, mesh=mesh, in_specs=in_specs, out_specs=out_specs, check_vma=False)
```

profile of v0, /device:TPU:0, one launch (start us, length us, event | category | flops | bytes accessed | tf_op | source)
XLA Modules:
  0.0 221.0 jit_solution(3574953310530504106)
XLA Ops:
  7.2 0.0 copy-start
  7.2 0.0 copy-start.5
  7.2 0.0 copy-start.4
  7.2 0.0 all-gather.5.cloned.1.call-start
  7.2 4.9 %slice_bitcast_fusion = bf16[128,128,128]{2,1,0:T(8,128)(2,1)} fusion(bf16[1,1,2,128,128,128]{5,4,3,2,1,0:T(8,128)(2,1)} %param.7), kind=kLoop, calls=%fused_computation.33 | loop fusion | bytes 8388608 | tf_op jit(solution)/shard_map/squeeze | solution.py:57
  12.1 0.5 collective-permute-start
  12.6 0.0 all-gather.5.cloned.1.call-update
  12.6 0.0 all-gather.3.cloned.1.call-start
  12.7 0.7 all-gather.3.cloned.1.call-update
  13.4 0.0 reduce-scatter.2.cloned.1.call-start
  13.4 0.0 copy-done.5
  13.5 0.6 slice.105
  14.1 0.0 copy-done.4
  14.1 0.6 fusion.98
  15.4 0.7 fusion.100
  16.0 54.2 %all-gather.5.cloned.1.call-done = bf16[1,512,1024]{2,1,0:T(8,128)(2,1)} async-done(((bf16[1,32,1024]{2,1,0:T(8,128)(2,1)}), bf16[1,512,1024]{2,1,0:T(8,128)(2,1)}) %all-gather.5.cloned.1.call-update) | async-done | bytes 1048592 | tf_op jit(solution)/shard_map/all_gather | solution.py:54
  70.3 1.0 dynamic-slice_bitcast_fusion
  71.2 0.1 collective-permute-start.2
  71.3 2.0 pad_maximum_fusion
  73.4 0.5 collective-permute-start.1
  74.5 0.1 collective-permute-done.1
  74.7 0.7 fusion.99
  78.5 14.5 %all-gather.3.cloned.1.call-done = bf16[1,512,1024]{2,1,0:T(8,128)(2,1)} async-done(((bf16[1,64,1024]{2,1,0:T(8,128)(2,1)}), bf16[1,512,1024]{2,1,0:T(8,128)(2,1)}) %all-gather.3.cloned.1.call-update) | async-done | bytes 1048592 | tf_op jit(solution)/shard_map/all_gather | solution.py:53
  93.0 1.0 dynamic-slice_bitcast_fusion.5
  93.9 0.0 collective-permute-done.2
  93.9 1.0 bitcast_select_fusion.1
  95.0 0.0 collective-permute-done
  95.0 3.9 %bitcast_select_fusion = bf16[128,128,128]{2,1,0:T(8,128)(2,1)S(1)} fusion(bf16[128,128,128]{2,1,0:T(8,128)(2,1)} %collective-permute-done, bf16[1,1,2,128,128,128]{5,4,3,2,1,0:T(8,128)(2,1)} %param.7, pred[]{:T(512)} %bitcast), kind=kLoop, calls=%fused_computation.16 | loop fusion | flops 2097152 | bytes 12582913 | tf_op jit(solution)/shard_map/jit(_where)/select_n | solution.py:61
  98.9 0.8 fusion.97
  99.7 1.3 fusion.47
  101.0 1.3 fusion.50
  102.3 1.3 fusion.53
  103.7 1.6 broadcast.9
  105.3 2.1 fusion.86
  107.4 57.5 %all-reduce.1 = bf16[512,1024]{1,0:T(8,128)(2,1)S(1)} all-reduce(f32[512,1024]{1,0:T(8,128)} %fusion.86), channel_id=1, replica_groups=mesh['ia'=4,'ja'=4,'ka'=2] {'ja','ka'}, use_global_device_ids=true, to_apply=%region_0.1 | all-reduce | flops 524288 | bytes 3145728 | tf_op jit(solution)/shard_map/psum | solution.py:71
  164.9 0.0 copy-done
  164.9 1.3 convolution_convert_fusion
  166.2 0.0 copy-start.3
  166.2 1.0 copy-done.3
  167.2 2.6 %fusion.35 = f32[128,1024]{1,0:T(8,128)S(1)} fusion(bf16[128,128,128]{2,1,0:T(8,128)(2,1)} %copy-done.1, bf16[32,1024]{1,0:T(8,128)(2,1)S(1)} %get-tuple-element.8, bf16[128,1024]{1,0:T(8,128)(2,1)S(1)} %bitcast_select_fusion.1), kind=kOutput, calls=%fused_computation.36 | convolution fusion | flops 1090519040 | bytes 5046272 | tf_op jit(solution)/shard_map/dot_general | solution.py:28
  169.8 1.3 fusion.38
  171.2 1.3 fusion.41
  172.5 1.6 broadcast_in_dim.9
  174.1 2.3 %fusion.77 = f32[1,512,1024]{2,1,0:T(8,128)} fusion(f32[1,512,1024]{2,1,0:T(8,128)} %broadcast_in_dim.9, s32[]{:T(128)S(6)} %select_n.47, f32[128,1024]{1,0:T(8,128)S(1)} %fusion.41, f32[128,1024]{1,0:T(8,128)S(1)} %fusion.38, f32[128,1024]{1,0:T(8,128)S(1)} %fusion.35, bf16[128,128,128]{2,1,0:T(8,128)(2,1)S(1)} %copy-done.2, ...), kind=kOutput, calls=%fused_computation.50 | convolution fusion | flops 1091043328 | bytes 6619144 | tf_op jit(solution)/shard_map/dot_general | solution.py:28
  176.4 0.0 reduce-scatter.2.cloned.1.call-update
  176.5 1.6 dynamic-slice_bitcast_fusion.1
  178.0 33.6 %reduce-scatter.2.cloned.1.call-done = f32[1,64,1024]{2,1,0:T(8,128)} async-done(((f32[1,512,1024]{2,1,0:T(8,128)}), f32[1,64,1024]{2,1,0:T(8,128)}) %reduce-scatter.2.cloned.1.call-update) | async-done | bytes 262160 | tf_op jit(solution)/shard_map/reduce_scatter | solution.py:84
  211.6 2.8 %fusion.89 = bf16[1,64,1024]{2,1,0:T(8,128)(2,1)} fusion(bf16[1024,1024]{1,0:T(8,128)(2,1)} %param.13, f32[1,64,1024]{2,1,0:T(8,128)} %reduce-scatter.2.cloned.1.call-done), kind=kOutput, calls=%fused_computation.55 | convolution fusion | flops 134348800 | bytes 2490368 | tf_op jit(solution)/shard_map/dot_general | solution.py:87
  (8 shorter events, 0.0 us)
Async XLA Ops:
  7.2 157.8 %copy-start = (bf16[1024,1024]{1,0:T(8,128)(2,1)S(1)}, bf16[1024,1024]{1,0:T(8,128)(2,1)}, u32[]{:S(2)}) copy-start(bf16[1024,1024]{1,0:T(8,128)(2,1)} %param.12) | copy-start | bytes 6291460
  7.2 6.3 %copy-start.5 = (s32[1,1,2]{2,1,0:T(1,128)S(1)}, s32[1,1,2]{2,1,0:T(1,128)}, u32[]{:S(2)}) copy-start(s32[1,1,2]{2,1,0:T(1,128)} %param.9) | copy-start | bytes 28
  7.2 6.9 %copy-start.4 = (s32[3,1,1,2]{0,3,2,1:T(2,128)S(1)}, s32[3,1,1,2]{0,3,2,1:T(2,128)}, u32[]{:S(2)}) copy-start(s32[3,1,1,2]{0,3,2,1:T(2,128)} %param.8) | copy-start | bytes 76
  7.2 63.1 %all-gather.5.cloned.1.call-start = ((), (), s32[]{:S(2)}) async-start(), calls=%async_computation.2 | async-start | bytes 1114112 | tf_op jit(solution)/shard_map/all_gather | solution.py:54
  12.1 82.9 %collective-permute-start = (bf16[128,128,128]{2,1,0:T(8,128)(2,1)}, bf16[128,128,128]{2,1,0:T(8,128)(2,1)}, u32[]{:S(2)}, u32[]{:S(2)}) collective-permute-start(bf16[128,128,128]{2,1,0:T(8,128)(2,1)} %slice_bitcast_fusion), channel_id=1, source_target_pairs={{1,0},{0,1},{3,2},{2,3},{5,4},{4,5},{7,6},{6,7},{9,8},{8,9},{11,10... | collective-permute-start | bytes 12582920 | tf_op jit(solution)/shard_map/ppermute | solution.py:13
  12.6 80.3 %all-gather.3.cloned.1.call-start = ((), (), s32[]{:S(2)}) async-start(), calls=%async_computation.1 | async-start | bytes 1179648 | tf_op jit(solution)/shard_map/all_gather | solution.py:53
  13.4 198.3 %reduce-scatter.2.cloned.1.call-start = ((), (), s32[]{:S(2)}) async-start(), calls=%async_computation.3 | async-start | bytes 2359296 | tf_op jit(solution)/shard_map/reduce_scatter | solution.py:84
  71.2 22.7 %collective-permute-start.2 = (bf16[128,1024]{1,0:T(8,128)(2,1)S(1)}, bf16[128,1024]{1,0:T(8,128)(2,1)S(1)}, u32[]{:S(2)}, u32[]{:S(2)}) collective-permute-start(bf16[128,1024]{1,0:T(8,128)(2,1)S(1)} %dynamic-slice_bitcast_fusion), channel_id=1, source_target_pairs={{1,0},{0,1},{3,2},{2,3},{5,4},{4,5},{7,6},{6,7},{9,8},{8,9},{11,10... | collective-permute-start | bytes 786440 | tf_op jit(solution)/shard_map/ppermute | solution.py:13
  73.4 1.3 collective-permute-start.1
  98.9 2.1 copy-start.1
  166.2 1.0 copy-start.3
  167.2 2.7 %copy-start.2 = (bf16[128,128,128]{2,1,0:T(8,128)(2,1)S(1)}, bf16[128,128,128]{2,1,0:T(8,128)(2,1)}, u32[]{:S(2)}) copy-start(bf16[128,128,128]{2,1,0:T(8,128)(2,1)} %copy-done.1) | copy-start | bytes 12582916
Sparse Core Ops, SparseCore 0:
  12.8 57.4 all-gather.4
  71.9 21.0 all-gather.2
  176.6 35.0 reduce-scatter.1
where the time goes:
time: 221 us
  waiting for transfers between devices  103 us (47%)
  blocking collectives  57.5 us (26%)
  between operations  18.5 us (8%)
  matrix products  17.8 us (8%)
  local copies, waits for them, and re-layouts  16 us (7%)
  other arithmetic  6.99 us (3%)
    psum x1, blocking collectives, body(): summed_rows = lax.psum(first_partial, ('ja', 'ka'))  57.5 us
    all_gather x1, waiting for transfers between devices, body(): lax.all_gather(third_factor, ('ia', 'ja'), axis=1, tiled=True)[0]  54.2 us
    reduce_scatter x1, waiting for transfers between devices, body(): lax.psum_scatter(second_partial[None], ('ia', 'ka'), scatter_dimension=1,...  33.6 us
    all_gather x1, waiting for transfers between devices, body(): lax.all_gather(second_factor, ('ia', 'ka'), axis=1, tiled=True)[0]  14.5 us
    dot_general x8, matrix products, block_products(): lax.dot_general(block_part, khatri, contraction, preferred_element_type=j...  13.7 us
    squeeze x1, local copies, waits for them, and re-layouts, body(): own_blocks[1]  4.87 us
  transfers between devices with their start and end apart: 6, of which 4 were waited for; matrix products, arithmetic and copies ran while one was open for 4% of the time, Pallas kernels for 0%

commit v1 on v0

--- a/solution.py
+++ b/solution.py
@@ -68,7 +68,7 @@
         tensor_block, pick_rows(second_rows, col_block, block_edge), layer_slab, 1
     )
     first_partial = place_rows(first_partial, contribution * weight, row_block)
-    summed_rows = lax.psum(first_partial, ("ja", "ka"))
+    summed_rows = jnp.sum(lax.all_gather(first_partial, ("ja", "ka")), axis=0)
     first_rows = jnp.dot(
         summed_rows.astype(jnp.bfloat16), inverse_first, preferred_element_type=jnp.float32
     ).astype(jnp.bfloat16)

time: 221 us -> 271 us (1.23)
  waiting for transfers between devices: 103 us -> 189 us
  blocking collectives: 57.5 us -> 0 us
  other arithmetic: 6.99 us -> 18.3 us
  local copies, waits for them, and re-layouts: 16 us -> 25 us
    all_gather x0 -> x1, waiting for transfers between devices: none -> 84.5 us  [body(): summed_rows = jnp.sum(lax.all_gather(first_partial, ('ja', 'ka')), axis=0)]
    psum x1 -> x0, blocking collectives: 57.5 us -> none  [body(): summed_rows = lax.psum(first_partial, ('ja', 'ka'))]
    slice x1 -> x2, local copies, waits for them, and re-layouts: 0.8 us -> 10 us  [the longest x1 5.35 us: body(): tensor_block = jnp.where(keep_own, own_blocks[0], arrived)]
    reduce_sum x0 -> x1, other arithmetic: none -> 7.94 us  [body(): summed_rows = jnp.sum(lax.all_gather(first_partial, ('ja', 'ka')), axis=0)]
    squeeze x1 -> x0, local copies, waits for them, and re-layouts: 4.87 us -> none  [body(): own_blocks[1]]
    unnamed x12 -> x17, local copies, waits for them, and re-layouts: 0.99 us -> 5.67 us
    select_n x1, other arithmetic: 3.91 us -> 7.31 us  [body(): tensor_block = jnp.where(keep_own, own_blocks[0], arrived)]
    all_gather x0 -> x2, local copies, waits for them, and re-layouts: none -> 3.19 us  [body(): summed_rows = jnp.sum(lax.all_gather(first_partial, ('ja', 'ka')), axis=0)]
  transfers between devices with their start and end apart: 6 -> 7, of which waited for: 4 -> 5; matrix products, arithmetic and copies ran while one was open for 4% -> 5% of each run, Pallas kernels for 0% -> 0%
where the time goes in v1:
time: 271 us; the launch traced here: 270 us
  waiting for transfers between devices  189 us (70%)
  local copies, waits for them, and re-layouts  25 us (9%)
  between operations  18.5 us (7%)
  other arithmetic  18.3 us (7%)
  matrix products  18 us (7%)
    all_gather x1, waiting for transfers between devices, body(): summed_rows = jnp.sum(lax.all_gather(first_partial, ('ja', 'ka')), axis=0)  84.5 us
    all_gather x1, waiting for transfers between devices, body(): lax.all_gather(third_factor, ('ia', 'ja'), axis=1, tiled=True)[0]  54 us
    reduce_scatter x1, waiting for transfers between devices, body(): lax.psum_scatter(second_partial[None], ('ia', 'ka'), scatter_dimension=1,...  34.7 us
    all_gather x1, waiting for transfers between devices, body(): lax.all_gather(second_factor, ('ia', 'ka'), axis=1, tiled=True)[0]  14.5 us
    dot_general x8, matrix products, block_products(): lax.dot_general(block_part, khatri, contraction, preferred_element_type=j...  14 us
    reduce_sum x1, other arithmetic, body(): summed_rows = jnp.sum(lax.all_gather(first_partial, ('ja', 'ka')), axis=0)  7.94 us
    select_n x1, other arithmetic, body(): tensor_block = jnp.where(keep_own, own_blocks[0], arrived)  7.31 us
    unnamed x17, local copies, waits for them, and re-layouts  5.67 us
  transfers between devices with their start and end apart: 7, of which 5 were waited for; matrix products, arithmetic and copies ran while one was open for 5% of the time, Pallas kernels for 0%

profile of v1, /device:TPU:0, one launch (start us, length us, event | category | flops | bytes accessed | tf_op | source)
XLA Modules:
  0.0 270.1 jit_solution(13673917645614490378)
XLA Ops:
  7.2 0.0 copy-start
  7.2 0.0 all-gather.6.cloned.1.call-start
  7.2 5.3 %fusion.101 = (bf16[1,1,1,128,128,128]{5,4,3,2,1,0:T(8,128)(2,1)}, bf16[1,1,1,128,128,128]{5,4,3,2,1,0:T(8,128)(2,1)S(1)}) fusion(bf16[1,1,2,128,128,128]{5,4,3,2,1,0:T(8,128)(2,1)} %param.7), kind=kLoop, calls=%fused_computation.78 | loop fusion | bytes 16777216 | tf_op jit(solution)/shard_map/slice | solution.py:61
  12.6 4.7 %copy.35 = bf16[1,1,1,128,128,128]{5,3,4,2,1,0:T(8,128)(2,1)} copy(bf16[1,1,1,128,128,128]{5,4,3,2,1,0:T(8,128)(2,1)S(1)} %get-tuple-element.3) | data formatting | bytes 8388608
  17.3 0.5 collective-permute-start
  17.8 0.0 all-gather.6.cloned.1.call-update
  17.8 0.0 all-gather.4.cloned.1.call-start
  17.8 0.7 all-gather.4.cloned.1.call-update
  18.5 0.2 all-gather.8.cloned.1.call-start
  18.8 0.6 slice.105
  19.4 0.6 fusion.103
  20.7 0.7 fusion.105
  21.4 54.0 %all-gather.6.cloned.1.call-done = bf16[1,512,1024]{2,1,0:T(8,128)(2,1)} async-done(((bf16[1,32,1024]{2,1,0:T(8,128)(2,1)}), bf16[1,512,1024]{2,1,0:T(8,128)(2,1)}) %all-gather.6.cloned.1.call-update) | async-done | bytes 1048592 | tf_op jit(solution)/shard_map/all_gather | solution.py:54
  75.4 1.0 dynamic-slice_bitcast_fusion
  76.4 0.1 collective-permute-start.2
  76.5 2.0 pad_maximum_fusion
  78.5 0.5 collective-permute-start.1
  79.7 0.1 collective-permute-done.1
  79.8 0.7 fusion.104
  83.7 14.5 %all-gather.4.cloned.1.call-done = bf16[1,512,1024]{2,1,0:T(8,128)(2,1)} async-done(((bf16[1,64,1024]{2,1,0:T(8,128)(2,1)}), bf16[1,512,1024]{2,1,0:T(8,128)(2,1)}) %all-gather.4.cloned.1.call-update) | async-done | bytes 1048592 | tf_op jit(solution)/shard_map/all_gather | solution.py:53
  98.1 1.0 dynamic-slice_bitcast_fusion.5
  99.1 0.0 collective-permute-done.2
  99.1 1.0 bitcast_select_fusion
  100.1 0.0 collective-permute-done
  100.1 7.3 %fusion.16 = bf16[128,128,128]{2,0,1:T(8,128)(2,1)S(1)} fusion(bf16[128,128,128]{2,0,1:T(8,128)(2,1)} %collective-permute-done, bf16[1,1,1,128,128,128]{5,4,3,2,1,0:T(8,128)(2,1)} %get-tuple-element.2, pred[]{:T(512)} %bitcast), kind=kLoop, calls=%fused_computation.18 | loop fusion | flops 2097152 | bytes 12582913 | tf_op jit(solution)/shard_map/jit(_where)/select_n | solution.py:61
  107.5 1.3 fusion.36
  108.8 1.3 fusion.39
  110.1 1.3 fusion.42
  111.5 1.6 all_gather.14.clone
  113.1 2.3 fusion.78
  115.4 0.0 all-gather.8.cloned.1.call-update
  115.4 0.3 reduce-scatter.2.cloned.1.call-start
  115.7 4.7 %fusion.102 = (bf16[32,128,128]{2,0,1:T(8,128)(2,1)}, bf16[32,128,128]{2,0,1:T(8,128)(2,1)}, bf16[32,128,128]{2,0,1:T(8,128)(2,1)}, bf16[32,128,128]{2,0,1:T(8,128)(2,1)}) fusion(bf16[128,128,128]{2,0,1:T(8,128)(2,1)} %copy-done.1), kind=kLoop, calls=%fused_computation.79 | loop fusion | bytes 8388608 | tf_op jit(solution)/shard_map/slice | solution.py:26
  120.4 84.5 %all-gather.8.cloned.1.call-done = f32[8,512,1024]{2,1,0:T(8,128)} async-done(((f32[1,512,1024]{2,1,0:T(8,128)}), f32[8,512,1024]{2,1,0:T(8,128)}) %all-gather.8.cloned.1.call-update) | async-done | bytes 16777232 | tf_op jit(solution)/shard_map/all_gather | solution.py:71
  204.9 7.9 %reduce_sum.9 = bf16[512,1024]{1,0:T(8,128)(2,1)S(1)} reduce(f32[8,512,1024]{2,1,0:T(8,128)} %all-gather.8.cloned.1.call-done, f32[]{:T(128)} %constant.22.clone.1), dimensions={0}, to_apply=%region_0.1 | reduce | flops 3670016 | bytes 17825796 | tf_op jit(solution)/shard_map/reduce_sum | solution.py:71
  212.8 1.3 convolution_convert_fusion
  214.1 0.9 copy-done.5
  215.1 2.6 fusion.48
  217.7 1.4 fusion.51
  219.1 0.0 copy-done.3
  219.2 0.0 copy-start.2
  219.2 1.4 fusion.54
  220.6 1.6 all_gather.14
  222.2 2.2 fusion.90
  224.4 0.0 reduce-scatter.2.cloned.1.call-update
  224.4 1.6 dynamic-slice_bitcast_fusion.1
  226.0 34.7 %reduce-scatter.2.cloned.1.call-done = f32[1,64,1024]{2,1,0:T(8,128)} async-done(((f32[1,512,1024]{2,1,0:T(8,128)}), f32[1,64,1024]{2,1,0:T(8,128)}) %reduce-scatter.2.cloned.1.call-update) | async-done | bytes 262160 | tf_op jit(solution)/shard_map/reduce_scatter | solution.py:84
  260.7 2.8 %fusion.93 = bf16[1,64,1024]{2,1,0:T(8,128)(2,1)} fusion(bf16[1024,1024]{1,0:T(8,128)(2,1)} %param.13, f32[1,64,1024]{2,1,0:T(8,128)} %reduce-scatter.2.cloned.1.call-done), kind=kOutput, calls=%fused_computation.57 | convolution fusion | flops 134348800 | bytes 2490368 | tf_op jit(solution)/shard_map/dot_general | solution.py:87
  (16 shorter events, 0.1 us)
Async XLA Ops:
  7.2 205.7 %copy-start = (bf16[1024,1024]{1,0:T(8,128)(2,1)S(1)}, bf16[1024,1024]{1,0:T(8,128)(2,1)}, u32[]{:S(2)}) copy-start(bf16[1024,1024]{1,0:T(8,128)(2,1)} %param.12) | copy-start | bytes 6291460
  7.2 68.2 %all-gather.6.cloned.1.call-start = ((), (), s32[]{:S(2)}) async-start(), calls=%async_computation.2 | async-start | bytes 1114112 | tf_op jit(solution)/shard_map/all_gather | solution.py:54
  12.6 6.2 %copy-start.7 = (s32[1,1,2]{2,1,0:T(1,128)S(1)}, s32[1,1,2]{2,1,0:T(1,128)}, u32[]{:S(2)}) copy-start(s32[1,1,2]{2,1,0:T(1,128)} %param.9) | copy-start | bytes 28
  12.6 6.8 %copy-start.6 = (s32[3,1,1,2]{0,3,2,1:T(2,128)S(1)}, s32[3,1,1,2]{0,3,2,1:T(2,128)}, u32[]{:S(2)}) copy-start(s32[3,1,1,2]{0,3,2,1:T(2,128)} %param.8) | copy-start | bytes 76
  17.3 82.9 %collective-permute-start = (bf16[128,128,128]{2,0,1:T(8,128)(2,1)}, bf16[128,128,128]{2,0,1:T(8,128)(2,1)}, u32[]{:S(2)}, u32[]{:S(2)}) collective-permute-start(bf16[128,128,128]{2,0,1:T(8,128)(2,1)} %bitcast.93), channel_id=1, source_target_pairs={{1,0},{0,1},{3,2},{2,3},{5,4},{4,5},{7,6},{6,7},{9,8},{8,9},{11,10... | collective-permute-start | bytes 12582920 | tf_op jit(solution)/shard_map/ppermute | solution.py:13
  17.8 80.3 %all-gather.4.cloned.1.call-start = ((), (), s32[]{:S(2)}) async-start(), calls=%async_computation.1 | async-start | bytes 1179648 | tf_op jit(solution)/shard_map/all_gather | solution.py:53
  18.5 186.3 %all-gather.8.cloned.1.call-start = ((), (), s32[]{:S(2)}) async-start(), calls=%async_computation.3 | async-start | bytes 18874368 | tf_op jit(solution)/shard_map/all_gather | solution.py:71
  76.4 22.7 %collective-permute-start.2 = (bf16[128,1024]{1,0:T(8,128)(2,1)S(1)}, bf16[128,1024]{1,0:T(8,128)(2,1)S(1)}, u32[]{:S(2)}, u32[]{:S(2)}) collective-permute-start(bf16[128,1024]{1,0:T(8,128)(2,1)S(1)} %dynamic-slice_bitcast_fusion), channel_id=1, source_target_pairs={{1,0},{0,1},{3,2},{2,3},{5,4},{4,5},{7,6},{6,7},{9,8},{8,9},{11,10... | collective-permute-start | bytes 786440 | tf_op jit(solution)/shard_map/ppermute | solution.py:13
  78.5 1.3 collective-permute-start.1
  107.4 5.6 %copy-start.1 = (bf16[128,128,128]{2,0,1:T(8,128)(2,1)}, bf16[128,128,128]{2,0,1:T(8,128)(2,1)S(1)}, u32[]{:S(2)}) copy-start(bf16[128,128,128]{2,0,1:T(8,128)(2,1)S(1)} %fusion.16) | copy-start | bytes 12582916
  115.4 145.3 %reduce-scatter.2.cloned.1.call-start = ((), (), s32[]{:S(2)}) async-start(), calls=%async_computation.4 | async-start | bytes 2359296 | tf_op jit(solution)/shard_map/reduce_scatter | solution.py:84
  214.1 1.0 copy-start.5
  215.1 2.6 copy-start.4
  217.7 1.4 copy-start.3
  219.2 3.0 %copy-start.2 = (bf16[32,128,128]{2,0,1:T(8,128)(2,1)S(1)}, bf16[32,128,128]{2,0,1:T(8,128)(2,1)}, u32[]{:S(2)}) copy-start(bf16[32,128,128]{2,0,1:T(8,128)(2,1)} %get-tuple-element.4) | copy-start | bytes 3145732
Sparse Core Ops, SparseCore 0:
  17.9 57.4 all-gather.5
  77.0 21.0 all-gather.3
  115.5 89.3 all-gather.7
  224.6 36.1 reduce-scatter.1
